TPU v7x, 32 devices: a whole 2x2x4 slice. The times are simulated.
32 devices in a mesh: dp: 8 (over z, x), mp: 4 (over y, core).
Axes of the slice: x: 2, y: 2, z: 4, core: 2. Of those that a mesh axis runs over, the one named last changes fastest.
Arguments:
- tokens: bfloat16 [16384, 512], P('dp'), may hold values from -6 to 6
- cotangent: bfloat16 [16384, 512], P('dp'), may hold values from -6 to 6
- bucket: int32 [16384, 1], P('dp'), may hold values from 0 to 7, as said below
- cell: int32 [16384], P('dp'), may hold values from 0 to 1, as said below
- features: bfloat16 [4, 64, 256], replicated, may hold values from -4 to 4
- qkv_weight: bfloat16 [3, 512, 512], P(None, None, 'mp'), may hold values from -0.25 to 0.25
- out_weight: bfloat16 [512, 512], P('mp'), may hold values from -1 to 1
- out_bias: float32 [512], replicated, may hold values from -3 to 3
- norm1_gain: float32 [512], replicated, may hold values from 0.25 to 1.75
- norm1_bias: float32 [512], replicated, may hold values from -3 to 3
- norm2_gain: float32 [512], replicated, may hold values from 0.25 to 1.75
- norm2_bias: float32 [512], replicated, may hold values from -3 to 3
- up_weight: bfloat16 [512, 2048], P(None, 'mp'), may hold values from -0.25 to 0.25
- up_bias: float32 [2048], P('mp'), may hold values from -3 to 3
- down_weight: bfloat16 [2048, 512], P('mp'), may hold values from -0.125 to 0.125
- down_bias: float32 [512], replicated, may hold values from -3 to 3
Outputs:
- output: bfloat16 [16384, 512], P('dp')
- grad_tokens: float32 [16384, 512], P('dp')
- grad_qkv_weight: float32 [3, 512, 512], P(None, None, 'mp')
- grad_out_weight: float32 [512, 512], P('mp')
- grad_out_bias: float32 [512], replicated
- grad_norm1_gain: float32 [512], replicated
- grad_norm1_bias: float32 [512], replicated
- grad_norm2_gain: float32 [512], replicated
- grad_norm2_bias: float32 [512], replicated
- grad_up_weight: float32 [512, 2048], P(None, 'mp')
- grad_up_bias: float32 [2048], P('mp')
- grad_down_weight: float32 [2048, 512], P('mp')
- grad_down_bias: float32 [512], replicated
Inputs may be any that keep to these rules, and one draw needn't show every extreme that they name: The 2048 rows of one device name every bucket at least once and one bucket at most 512 times, and every device names some bucket exactly 512 times. In every bucket one cell, drawn from the seed, holds tokens from every device.
All inputs are finite; a program needn't handle non-finite values.
Results may differ from a plain program's by a relative error of at most 0.012.
The roundings to bfloat16 on the way count: a program that leaves them out, or rounds other values in their place, can miss the bound.
Values may be sent and summed in bfloat16 or wider, within the bound.
A program may use at most 192 MiB of HBM per device.

v0:
```python
import jax
import jax.numpy as jnp
from jax import lax
from jax.sharding import PartitionSpec as P

HD = 64
FEATS = 4
STEP = 5
SEG = 2


EXACT_PRECISION = lax.Precision.HIGHEST


def layer_norm(values, norm_gain, norm_bias):
    average = jnp.mean(values, -1, keepdims=True)
    centred = values - average
    spread = jnp.mean(centred * centred, -1, keepdims=True)
    return centred * lax.rsqrt(spread + 1e-05) * norm_gain + norm_bias


def exact_gelu(values):
    return jax.nn.gelu(values, approximate=False)


def rounded(values):
    return lax.optimization_barrier(values.astype(jnp.bfloat16)).astype(jnp.float32)


def feature_map(rows, feature_rows):
    scale = HD ** (-0.25)
    projected = (
        jnp.einsum("thd,dm->thm", rows, feature_rows, preferred_element_type=jnp.float32) * scale
    )
    widened = rows.astype(jnp.float32)
    squares = 0.5 * scale * scale * jnp.sum(widened * widened, -1, keepdims=True)
    return jnp.exp(projected - squares)


def feature_back(rows, feature_rows, feats, grad_feats):
    scale = HD ** (-0.25)
    weighted = grad_feats * feats
    widened = rows.astype(jnp.float32)
    spread_back = jnp.einsum(
        "thm,dm->thd", weighted, feature_rows.astype(jnp.float32), precision=EXACT_PRECISION
    )
    return scale * spread_back - scale * scale * widened * jnp.sum(weighted, -1, keepdims=True)


def per_device(
    tokens,
    cotangent,
    bucket,
    cell,
    features,
    qkv_weight,
    out_weight,
    out_bias,
    norm1_gain,
    norm1_bias,
    norm2_gain,
    norm2_bias,
    up_weight,
    up_bias,
    down_weight,
    down_bias,
):
    bucket_count = lax.axis_size("dp")
    token_count = tokens.shape[0]
    local_width = qkv_weight.shape[2]
    heads_local = local_width // HD
    capacity = 2 * token_count // bucket_count
    slots = bucket_count * capacity
    target = bucket[:, 0]
    membership = (target[:, None] == jnp.arange(bucket_count, dtype=jnp.int32)[None, :]).astype(
        jnp.int32
    )
    rank_within = jnp.sum(jnp.cumsum(membership, 0) * membership, 1) - 1
    slot_index = target * capacity + rank_within

    def to_slots(rows):
        return jnp.zeros((slots,) + rows.shape[1:], rows.dtype).at[slot_index].set(rows)

    def home_rows(partial_rows):
        returned = lax.all_to_all(partial_rows, "dp", split_axis=0, concat_axis=0, tiled=True)
        return lax.psum(returned[slot_index], "mp").astype(jnp.bfloat16)

    def over_units(partial_rows):
        return lax.psum(partial_rows, "mp")

    residual = tokens.astype(jnp.float32)
    normed, norm1_back = jax.vjp(layer_norm, residual, norm1_gain, norm1_bias)
    normed_low = normed.astype(jnp.bfloat16)
    cell_labels = (cell + 1).astype(jnp.bfloat16)
    received, slot_cells = (
        lax.all_to_all(to_slots(normed_low), "dp", split_axis=0, concat_axis=0, tiled=True),
        lax.all_to_all(to_slots(cell_labels), "dp", split_axis=0, concat_axis=0, tiled=True),
    )
    projected = jnp.einsum(
        "td,cde->tce", received, qkv_weight, preferred_element_type=jnp.float32
    ).astype(jnp.bfloat16)
    labels_wide = slot_cells.astype(jnp.float32)
    cell_masks = (
        labels_wide[:, None] == jnp.arange(1, SEG + 1, dtype=jnp.float32)[None, :]
    ).astype(jnp.float32)
    occupied = jnp.sum(cell_masks, 1)
    masks_low = cell_masks.astype(jnp.bfloat16)
    query = projected[:, 0].reshape(slots, heads_local, HD)
    key_rows = projected[:, 1].reshape(slots, heads_local, HD)
    value_matrix_rows = projected[:, 2].reshape(slots, heads_local, HD)
    feature_rows = features[STEP % FEATS]
    query_wide = feature_map(query, feature_rows)
    key_wide = feature_map(key_rows, feature_rows)
    query_feature_map = query_wide.astype(jnp.bfloat16)
    key_feature_map = key_wide.astype(jnp.bfloat16)
    attention_numerator = jnp.zeros((slots, heads_local, HD), jnp.float32)
    denominator = jnp.broadcast_to((1.0 - occupied)[:, None], (slots, heads_local))
    cell_states = []
    cell_totals = []
    for part_index in range(SEG):
        weight_col = cell_masks[:, part_index]
        cell_memory_state = jnp.einsum(
            "ciu,cib->iub",
            key_feature_map * masks_low[:, part_index, None, None],
            value_matrix_rows,
            preferred_element_type=jnp.float32,
        ).astype(jnp.bfloat16)
        cell_total = jnp.einsum(
            "thm,t->hm",
            key_feature_map,
            masks_low[:, part_index],
            preferred_element_type=jnp.float32,
        )
        attention_numerator = attention_numerator + weight_col[:, None, None] * jnp.einsum(
            "fba,bay->fby", query_feature_map, cell_memory_state, preferred_element_type=jnp.float32
        )
        denominator = denominator + weight_col[:, None] * jnp.einsum(
            "thm,hm->th",
            query_feature_map,
            cell_total,
            precision=EXACT_PRECISION,
            preferred_element_type=jnp.float32,
        )
        cell_states.append(cell_memory_state)
        cell_totals.append(cell_total)
    attention = (
        (attention_numerator / denominator[..., None])
        .reshape(slots, local_width)
        .astype(jnp.bfloat16)
    )
    branch = home_rows(jnp.dot(attention, out_weight, preferred_element_type=jnp.float32))
    midstream = residual + branch.astype(jnp.float32) + out_bias
    normed2, norm2_back = jax.vjp(layer_norm, midstream, norm2_gain, norm2_bias)
    normed2_low = normed2.astype(jnp.bfloat16)
    preact = jnp.dot(normed2_low, up_weight, preferred_element_type=jnp.float32) + up_bias
    active, gelu_back = jax.vjp(exact_gelu, preact)
    active_low = active.astype(jnp.bfloat16)
    branch_out = over_units(jnp.dot(active_low, down_weight, preferred_element_type=jnp.float32))
    output = (midstream + branch_out + down_bias).astype(jnp.bfloat16)
    upstream = cotangent.astype(jnp.float32)
    contract_rows = (((0,), (0,)), ((), ()))
    grad_down_bias = jnp.sum(upstream, 0)
    grad_down_weight = lax.dot_general(
        active_low, cotangent, contract_rows, preferred_element_type=jnp.float32
    )
    (grad_preact,) = gelu_back(
        jnp.dot(cotangent, down_weight.T, preferred_element_type=jnp.float32)
    )
    grad_preact_low = grad_preact.astype(jnp.bfloat16)
    grad_up_bias = jnp.sum(grad_preact_low.astype(jnp.float32), 0)
    grad_up_weight = lax.dot_general(
        normed2_low, grad_preact_low, contract_rows, preferred_element_type=jnp.float32
    )
    grad_normed2 = over_units(
        jnp.dot(grad_preact_low, up_weight.T, preferred_element_type=jnp.float32)
    )
    grad_mid_norm, grad_norm2_gain, grad_norm2_bias = norm2_back(grad_normed2)
    grad_midstream = upstream + grad_mid_norm
    grad_out_bias = jnp.sum(grad_midstream, 0)
    grad_branch = grad_midstream.astype(jnp.bfloat16)
    arrived = lax.all_to_all(to_slots(grad_branch), "dp", split_axis=0, concat_axis=0, tiled=True)
    grad_out_weight = lax.dot_general(
        attention, arrived, contract_rows, preferred_element_type=jnp.float32
    )
    grad_attention = rounded(jnp.dot(arrived, out_weight.T, preferred_element_type=jnp.float32))
    grad_attention = grad_attention.reshape(slots, heads_local, HD)
    grad_numerator = grad_attention / denominator[..., None]
    grad_denominator = -jnp.sum(grad_attention * attention_numerator, -1) / (
        denominator * denominator
    )
    grad_query_feat = jnp.zeros((slots, heads_local, query_feature_map.shape[2]), jnp.float32)
    grad_key_feat = jnp.zeros_like(grad_query_feat)
    grad_value = jnp.zeros((slots, heads_local, HD), jnp.float32)
    for part_index in range(SEG):
        weight_col = cell_masks[:, part_index]
        numer_masked = grad_numerator * weight_col[:, None, None]
        denom_masked = grad_denominator * weight_col[:, None]
        grad_state = jnp.einsum(
            "ciu,cib->iub",
            query_feature_map,
            numer_masked,
            precision=EXACT_PRECISION,
            preferred_element_type=jnp.float32,
        )
        grad_total = jnp.einsum(
            "thm,th->hm",
            query_feature_map,
            denom_masked,
            precision=EXACT_PRECISION,
            preferred_element_type=jnp.float32,
        )
        grad_query_feat = (
            grad_query_feat
            + jnp.einsum(
                "peo,exo->pex",
                numer_masked,
                cell_states[part_index],
                precision=EXACT_PRECISION,
                preferred_element_type=jnp.float32,
            )
            + denom_masked[..., None] * cell_totals[part_index][None]
        )
        grad_key_feat = grad_key_feat + weight_col[:, None, None] * (
            jnp.einsum(
                "peo,exo->pex",
                value_matrix_rows,
                grad_state,
                precision=EXACT_PRECISION,
                preferred_element_type=jnp.float32,
            )
            + grad_total[None]
        )
        grad_value = grad_value + weight_col[:, None, None] * jnp.einsum(
            "fba,bay->fby",
            key_feature_map,
            grad_state,
            precision=EXACT_PRECISION,
            preferred_element_type=jnp.float32,
        )
    grad_query = feature_back(query, feature_rows, query_wide, grad_query_feat)
    grad_key = feature_back(key_rows, feature_rows, key_wide, grad_key_feat)
    grad_projected = jnp.stack(
        [
            grad_query.reshape(slots, local_width),
            grad_key.reshape(slots, local_width),
            grad_value.reshape(slots, local_width),
        ],
        1,
    ).astype(jnp.bfloat16)
    grad_qkv_weight = jnp.einsum(
        "td,tce->cde", received, grad_projected, preferred_element_type=jnp.float32
    )
    grad_normed = home_rows(
        jnp.einsum("tce,cde->td", grad_projected, qkv_weight, preferred_element_type=jnp.float32)
    )
    grad_residual, grad_norm1_gain, grad_norm1_bias = norm1_back(grad_normed.astype(jnp.float32))
    grad_tokens = grad_midstream + grad_residual
    summed = lax.psum(
        (
            grad_qkv_weight,
            grad_out_weight,
            grad_out_bias,
            grad_norm1_gain,
            grad_norm1_bias,
            grad_norm2_gain,
            grad_norm2_bias,
            grad_up_weight,
            grad_up_bias,
            grad_down_weight,
            grad_down_bias,
        ),
        "dp",
    )
    return (
        output,
        grad_tokens,
        summed[0],
        summed[1],
        summed[2],
        summed[3],
        summed[4],
        summed[5],
        summed[6],
        summed[7],
        summed[8],
        summed[9],
        summed[10],
    )


def solution(mesh):
    return jax.shard_map(
        per_device,
        mesh=mesh,
        in_specs=(
            P("dp", None),
            P("dp", None),
            P("dp", None),
            P("dp"),
            P(),
            P(None, None, "mp"),
            P("mp", None),
            P(),
            P(),
            P(),
            P(),
            P(),
            P(None, "mp"),
            P("mp"),
            P("mp", None),
            P(),
        ),
        out_specs=(
            P("dp", None),
            P("dp", None),
            P(None, None, "mp"),
            P("mp", None),
            P(),
            P(),
            P(),
            P(),
            P(),
            P(None, "mp"),
            P("mp"),
            P("mp", None),
            P(),
        ),
        check_vma=False,
    )
```

profile of v0, /device:TPU:12, one launch (start us, length us, event | category | flops | bytes accessed | tf_op | source)
XLA Modules:
  0.0 1300.8 jit_solution(10532565975702089205)
XLA Ops:
  13.1 14.6 %scatter_custom_fusion = bf16[4096]{0:T(1024)(128)(2,1)S(1)} fusion(s32[2048]{0:T(1024)S(1)} %bitcast.227, bf16[2048]{0:T(1024)(128)(2,1)S(1)} %add_convert_fusion.3, bf16[]{:T(256)} %constant.43.clone.1), kind=kCustom, calls=%fused_computation.181 | custom fusion | bytes 8194 | tf_op jit(solution)/shard_map/scatter | solution.py:82
  29.5 6.3 all-to-all-start
  39.4 13.3 %scatter_custom_fusion.1 = bf16[4096,512]{1,0:T(8,128)(2,1)} fusion(s32[2048]{0:T(1024)S(1)} %bitcast.228, bf16[2048,512]{1,0:T(8,128)(2,1)S(1)} %copy-done.7, f32[512]{0:T(512)S(1)} %copy-done.52, f32[512]{0:T(512)S(1)} %copy-done.48, f32[2048]{0:T(1024)S(1)} %fusion.100, f32[2048]{0:T(1024)S(1)} %broadcast_multiply_fusion.7, bf16[]{:T(256)} %constant.43.clone.1), kind=kCustom, calls=%fused_computation.89 | custom fusion | flops 6291456 | bytes 6311938 | tf_op jit(solution)/shard_map/scatter | solution.py:82
  52.7 6.4 all-to-all-start.1
  59.7 89.3 %all-to-all-done.1 = bf16[8,512,512]{2,1,0:T(8,128)(2,1)} async-done(((bf16[8,512,512]{2,1,0:T(8,128)(2,1)}), bf16[8,512,512]{2,1,0:T(8,128)(2,1)}, u32[]{:S(2)}, u32[]{:S(2)}) %all-to-all-start.1) | async-done | bytes 4194336 | tf_op jit(solution)/shard_map/all_to_all | solution.py:96
  149.0 4.0 fusion.120
  154.4 5.1 fusion.2
  165.0 5.1 fusion.3
  171.8 11.8 fusion.106
  184.6 2.4 divide_convert_fusion
  188.4 4.6 fusion.65
  193.0 7.4 all-to-all-start.2
  200.5 179.7 %all-to-all-done.2 = f32[8,512,512]{2,1,0:T(8,128)} async-done(((f32[8,512,512]{2,1,0:T(8,128)}), f32[8,512,512]{2,1,0:T(8,128)}, u32[]{:S(2)}, u32[]{:S(2)}) %all-to-all-start.2) | async-done | bytes 8388640 | tf_op jit(solution)/shard_map/all_to_all | solution.py:85
  380.2 12.9 gather_fusion
  393.1 76.6 %all-reduce.11 = bf16[2048,512]{1,0:T(8,128)(2,1)} all-reduce(f32[2048,512]{1,0:T(8,128)} %gather_fusion), channel_id=1, replica_groups=mesh['dp'=8,'mp'=4] {'mp'}, use_global_device_ids=true, to_apply=%region_10.11 | all-reduce | flops 1048576 | bytes 6291456 | tf_op jit(solution)/shard_map/psum | solution.py:86
  469.7 2.5 fusion.35
  476.5 10.6 convert_reduce_fusion.3
  488.5 3.2 fusion.122
  491.7 3.2 fusion.121
  494.9 153.7 %all-reduce.10.cloned.1.call-done = (f32[2048,512]{1,0:T(8,128)}, f32[2048,512]{1,0:T(8,128)}) async-done(((f32[2048,512]{1,0:T(8,128)}, f32[2048,512]{1,0:T(8,128)}), (f32[2048,512]{1,0:T(8,128)}, f32[2048,512]{1,0:T(8,128)})) %all-reduce.10.cloned.1.call-update) | async-done | bytes 8388624 | tf_op jit(solution)/shard_map/psum | solution.py:89
  648.6 4.6 multiply_reduce_fusion
  654.5 2.7 fusion.114
  657.3 13.7 %scatter_custom_fusion.2 = bf16[4096,512]{1,0:T(8,128)(2,1)} fusion(s32[2048]{0:T(1024)S(1)} %bitcast.230, bf16[]{:T(256)} %constant.43.clone.1, bf16[2048,512]{1,0:T(8,128)(2,1)S(1)} %copy-done.27, f32[2048,512]{1,0:T(8,128)} %get-tuple-element.82, f32[2048]{0:T(1024)S(1)} %negate_multiply_fusion.2), kind=kCustom, calls=%fused_computation.91 | custom fusion | flops 4194304 | bytes 10493954 | tf_op jit(solution)/shard_map/scatter | solution.py:82
  670.9 98.8 %all_to_all.55 = bf16[8,512,512]{2,1,0:T(8,128)(2,1)S(1)} all-to-all(bf16[8,512,512]{2,1,0:T(8,128)(2,1)} %bitcast.189), channel_id=1, replica_groups=mesh['dp'=8,'mp'=4] {'dp'}, dimensions={0} | all-to-all | bytes 8388608 | tf_op jit(solution)/shard_map/all_to_all | solution.py:181
  778.2 3.9 fusion.51
  782.1 3.9 fusion.54
  786.1 2.3 convolution_multiply_fusion.1
  788.4 5.7 fusion.123
  794.1 5.9 fusion.56
  800.0 3.3 fusion.86
  803.4 3.4 fusion.84
  806.7 3.3 fusion.16
  812.3 10.6 fusion.118
  822.9 4.7 fusion.15
  829.9 10.4 fusion.119
  840.4 3.7 fusion.14
  845.7 7.2 fusion.58
  852.9 5.8 all-to-all-start.4
  858.7 4.6 fusion.125
  863.3 2.4 fusion.110
  867.7 4.9 convolution_bitcast_fusion
  872.6 275.5 %all-reduce.8.cloned.1.call-done = (f32[3,512,128]{1,2,0:T(8,128)}, f32[128,512]{1,0:T(8,128)}, f32[512,512]{1,0:T(8,128)}, f32[512,512]{1,0:T(8,128)}) async-done(((f32[3,512,128]{1,2,0:T(8,128)}, f32[128,512]{1,0:T(8,128)}, f32[512,512]{1,0:T(8,128)}, f32[512,512]{1,0:T(8,128)}), (f32[3,512,128]{1,2,0:T(8,128)}, f32[128,512]{1,0:T(8,128)}, f32[512,512]{1,0:T(8,128)}, ...) | async-done | bytes 3145744 | tf_op jit(solution)/shard_map/psum | solution.py:258
  1150.4 12.9 gather_fusion.1
  1163.2 76.8 %all-reduce.12 = bf16[2048,512]{1,0:T(8,128)(2,1)} all-reduce(f32[2048,512]{1,0:T(8,128)} %gather_fusion.1), channel_id=1, replica_groups=mesh['dp'=8,'mp'=4] {'mp'}, use_global_device_ids=true, to_apply=%region_21.22 | all-reduce | flops 1048576 | bytes 6291456 | tf_op jit(solution)/shard_map/psum | solution.py:86
  1240.1 3.4 convert_reduce_fusion
  1243.6 3.6 fusion.24
  1247.2 7.5 convert_reduce_fusion.2
  1254.7 33.5 %all-reduce = (f32[512]{0:T(512)}, f32[512]{0:T(512)}, f32[512]{0:T(512)}, f32[512]{0:T(512)}, f32[512]{0:T(512)}, /*index=5*/f32[512]{0:T(512)}, f32[512]{0:T(512)}) all-reduce(f32[512]{0:T(512)S(1)} %get-tuple-element.58, f32[512]{0:T(512)S(1)} %get-tuple-element.54, ...), channel_id=1, replica_groups=mesh['dp'=8,'mp'=4] {'dp'}, use_global_device_ids=true, to_apply=%region_27.28 | all-reduce | flops 3584 | bytes 28672 | tf_op jit(solution)/shard_map/psum | solution.py:258
  (185 shorter events, 53.6 us)
Async XLA Ops:
  7.2 468.3 %copy-start = (bf16[512,512]{1,0:T(8,128)(2,1)S(1)}, bf16[512,512]{1,0:T(8,128)(2,1)}, u32[]{:S(2)}) copy-start(bf16[512,512]{1,0:T(8,128)(2,1)} %param.30) | copy-start | bytes 1572868
  7.2 30.5 %copy-start.7 = (bf16[2048,512]{1,0:T(8,128)(2,1)S(1)}, bf16[2048,512]{1,0:T(8,128)(2,1)}, u32[]{:S(2)}) copy-start(bf16[2048,512]{1,0:T(8,128)(2,1)} %param.16) | copy-start | bytes 6291460
  7.2 32.2 %copy-start.48 = (f32[512]{0:T(512)S(1)}, f32[512]{0:T(512)}, u32[]{:S(2)}) copy-start(f32[512]{0:T(512)} %param.24) | copy-start | bytes 6148
  7.2 32.1 %copy-start.52 = (f32[512]{0:T(512)S(1)}, f32[512]{0:T(512)}, u32[]{:S(2)}) copy-start(f32[512]{0:T(512)} %param.25) | copy-start | bytes 6148
  29.5 23.2 %all-to-all-start = ((bf16[8,2,256]{2,1,0:T(2,128)(2,1)}), bf16[8,2,256]{2,1,0:T(2,128)(2,1)S(1)}, u32[]{:S(2)}, u32[]{:S(2)}) async-start(bf16[8,2,256]{2,1,0:T(2,128)(2,1)} %reshape.249), calls=%async_computation | async-start | bytes 16384 | tf_op jit(solution)/shard_map/all_to_all | solution.py:97
  37.7 14.9 %copy-start.38 = (f32[2048]{0:T(1024)}, f32[2048]{0:T(1024)S(1)}, u32[]{:S(2)}) copy-start(f32[2048]{0:T(1024)S(1)} %broadcast_multiply_fusion.7) | copy-start | bytes 24580
  39.4 13.3 %copy-start.42 = (f32[2048]{0:T(1024)}, f32[2048]{0:T(1024)S(1)}, u32[]{:S(2)}) copy-start(f32[2048]{0:T(1024)S(1)} %fusion.100) | copy-start | bytes 24580
  52.7 6.4 copy-start.36
  52.7 96.3 %all-to-all-start.1 = ((bf16[8,512,512]{2,1,0:T(8,128)(2,1)}), bf16[8,512,512]{2,1,0:T(8,128)(2,1)}, u32[]{:S(2)}, u32[]{:S(2)}) async-start(bf16[8,512,512]{2,1,0:T(8,128)(2,1)} %bitcast.188), calls=%async_computation.1 | async-start | bytes 8388608 | tf_op jit(solution)/shard_map/all_to_all | solution.py:96
  153.7 5.8 copy-start.19
  153.7 9.9 copy-start.25
  153.7 11.2 copy-start.17
  159.5 4.1 copy-start.9
  170.1 14.5 %copy-start.2 = (bf16[4096,2,256]{0,2,1:T(8,128)(2,1)}, bf16[4096,2,256]{0,2,1:T(8,128)(2,1)S(1)}, u32[]{:S(2)}) copy-start(bf16[4096,2,256]{0,2,1:T(8,128)(2,1)S(1)} %get-tuple-element.100) | copy-start | bytes 12582916
  184.6 3.8 copy-start.35
  193.0 187.2 %all-to-all-start.2 = ((f32[8,512,512]{2,1,0:T(8,128)}), f32[8,512,512]{2,1,0:T(8,128)}, u32[]{:S(2)}, u32[]{:S(2)}) async-start(f32[8,512,512]{2,1,0:T(8,128)} %fusion.65), calls=%async_computation.2 | async-start | bytes 16777216 | tf_op jit(solution)/shard_map/all_to_all | solution.py:85
  200.5 448.2 %all-reduce.10.cloned.1.call-start = ((), (), s32[]{:S(2)}) async-start(), calls=%async_computation.6 | async-start | bytes 16777216 | tf_op jit(solution)/shard_map/psum | solution.py:89
  393.1 76.6 %copy-start.50 = (f32[512]{0:T(512)S(1)}, f32[512]{0:T(512)}, u32[]{:S(2)}) copy-start(f32[512]{0:T(512)} %param.23) | copy-start | bytes 6148
  469.7 2.5 copy-start.15
  473.4 3.1 copy-start.27
  473.4 3.1 copy-start.53
  488.3 3.5 copy-start.24
  648.6 4.7 copy-start.5
  648.6 5.9 copy-start.21
  775.4 2.8 copy-start.3
  782.1 3.9 copy-start.10
  812.3 10.7 copy-start.20
  829.9 10.4 copy-start.18
  840.4 5.3 copy-start.31
  840.4 5.3 copy-start.37
  852.9 297.5 %all-to-all-start.4 = ((f32[8,512,512]{2,1,0:T(8,128)}), f32[8,512,512]{2,1,0:T(8,128)}, u32[]{:S(2)}, u32[]{:S(2)}) async-start(f32[8,512,512]{2,1,0:T(8,128)} %bitcast.194), calls=%async_computation.4 | async-start | bytes 16777216 | tf_op jit(solution)/shard_map/all_to_all | solution.py:85
  858.7 4.6 copy-start.23
  858.7 289.4 %all-reduce.8.cloned.1.call-start = ((), (), s32[]{:S(2)}) async-start(), calls=%async_computation.5 | async-start | bytes 6291456 | tf_op jit(solution)/shard_map/psum | solution.py:258
  858.7 4.6 copy-start.6
  863.3 2.5 copy-start.12
  863.3 2.7 copy-start.29
  1163.2 76.9 %copy-start.8 = (bf16[2048,512]{1,0:T(8,128)(2,1)S(1)}, bf16[2048,512]{1,0:T(8,128)(2,1)}, u32[]{:S(2)}) copy-start(bf16[2048,512]{1,0:T(8,128)(2,1)} %param.16) | copy-start | bytes 6291460
  1163.2 76.9 %copy-start.39 = (f32[2048]{0:T(1024)S(1)}, f32[2048]{0:T(1024)}, u32[]{:S(2)}) copy-start(f32[2048]{0:T(1024)} %copy-done.38) | copy-start | bytes 24580
  1163.2 76.9 %copy-start.49 = (f32[512]{0:T(512)S(1)}, f32[512]{0:T(512)}, u32[]{:S(2)}) copy-start(f32[512]{0:T(512)} %param.24) | copy-start | bytes 6148
  1163.2 80.3 %copy-start.46 = (f32[2048]{0:T(1024)S(1)}, f32[2048]{0:T(1024)}, u32[]{:S(2)}) copy-start(f32[2048]{0:T(1024)} %copy-done.45) | copy-start | bytes 24580
  1163.2 80.3 %copy-start.43 = (f32[2048]{0:T(1024)S(1)}, f32[2048]{0:T(1024)}, u32[]{:S(2)}) copy-start(f32[2048]{0:T(1024)} %copy-done.42) | copy-start | bytes 24580
  1240.1 7.1 copy-start.13
  1240.1 7.1 copy-start.14
  1240.1 7.1 copy-start.16
  1240.1 7.1 copy-start.51
  1240.1 7.1 copy-start.54
  1247.2 41.0 %copy-start.40 = (f32[128,512]{1,0:T(8,128)S(1)}, f32[128,512]{1,0:T(8,128)}, u32[]{:S(2)}) copy-start(f32[128,512]{1,0:T(8,128)} %get-tuple-element.113) | copy-start | bytes 786436
  1247.2 46.3 %copy-start.1 = (bf16[512,512]{1,0:T(8,128)(2,1)S(1)}, bf16[512,512]{1,0:T(8,128)(2,1)}, u32[]{:S(2)}) copy-start(bf16[512,512]{1,0:T(8,128)(2,1)} %param.30) | copy-start | bytes 1572868
  (13 other events, 19.1 us)
Sparse Core Ops, SparseCore 0:
  495.1 153.5 all-reduce.9
  872.7 275.3 all-reduce.7
where the time goes:
time: 1320 us; the launch traced here: 1300 us
  waiting for transfers between devices  698 us (53%)
  blocking collectives  286 us (22%)
  matrix products  143 us (11%)
  other arithmetic  66.3 us (5%)
  local copies, waits for them, and re-layouts  66.1 us (5%)
  starting transfers between devices  25.8 us (2%)
  between operations  15.4 us (1%)
    psum x1, waiting for transfers between devices, per_device(): lax.psum((grad_qkv_weight, grad_out_weight, grad_out_bias, grad_norm1_gai...  275 us
    all_to_all x2, waiting for transfers between devices, home_rows(): lax.all_to_all(partial_rows, 'dp', split_axis=0, concat_axis=0, tiled=True)  180 us
    psum x1, waiting for transfers between devices, over_units(): return lax.psum(partial_rows, 'mp')  154 us
    psum x2, blocking collectives, home_rows(): return lax.psum(returned[slot_index], 'mp').astype(jnp.bfloat16)  153 us
    all_to_all x1, blocking collectives, per_device(): lax.all_to_all(to_slots(grad_branch), 'dp', split_axis=0, concat_axis=0,...  98.8 us
    all_to_all x1, waiting for transfers between devices, per_device(): lax.all_to_all(to_slots(normed_low), 'dp', split_axis=0, concat_axis=0, t...  89.3 us
    psum x1, blocking collectives, per_device(): lax.psum((grad_qkv_weight, grad_out_weight, grad_out_bias, grad_norm1_gai...  33.5 us
    scatter x2, other arithmetic, to_slots(): jnp.zeros((slots,) + rows.shape[1:], rows.dtype).at[slot_index].set(rows)  26.9 us
  transfers between devices with their start and end apart: 6, of which 4 were waited for; matrix products, arithmetic and copies ran while one was open for 2% of the time, Pallas kernels for 0%

commit v1 on v0

v1 whole, which is shorter than its diff:
```python
import functools
from types import SimpleNamespace

import jax
import jax.numpy as jnp
from jax import lax
from jax.experimental import pallas as pl
from jax.experimental.pallas import tpu as pltpu
from jax.sharding import PartitionSpec as P

HD = 64
FEATS = 4
STEP = 5
SEG = 2
PAD = 8
SCALE = HD**-0.25
HALF_SQUARE = 0.5 * SCALE * SCALE
EPS = 1e-05

BF = jnp.bfloat16
F32 = jnp.float32
MESH = pl.DeviceIdType.MESH
LANES = 128
TILE = 256


def dot(a, b):
    return jnp.dot(a, b, preferred_element_type=F32)


def dot_nt(a, b):
    return lax.dot_general(a, b, (((1,), (1,)), ((), ())), preferred_element_type=F32)


def dot_tn(a, b):
    return lax.dot_general(a, b, (((0,), (0,)), ((), ())), preferred_element_type=F32)


def lane(shape):
    return lax.broadcasted_iota(jnp.int32, shape, len(shape) - 1)


def roll_half(x):
    return pltpu.roll(x, HD, 1)


def loop(count, body, unroll=False):
    if unroll or count <= 4:
        for i in range(count):
            body(i)
    else:

        def step(i, carry):
            body(i)
            return carry

        lax.fori_loop(0, count, step, 0)


def rows_of(i, size):
    if isinstance(i, int):
        return pl.ds(i * size, size)
    return pl.ds(pl.multiple_of(i * size, size), size)


def normalised(values):
    average = jnp.mean(values, -1, keepdims=True)
    centred = values - average
    spread = jnp.mean(centred * centred, -1, keepdims=True)
    scale = lax.rsqrt(spread + EPS)
    return centred * scale, scale


def norm_back(upstream, hat, scale, gain):
    e = gain * upstream
    return (
        e
        - jnp.mean(e, -1, keepdims=True)
        - hat * jnp.mean(e * hat, -1, keepdims=True)
    ) * scale


def round_up(a, b):
    return (a + b - 1) // b * b


class Plan:
    def __init__(self, n, nm, tokens, width, local, feats, hidden):
        self.n, self.nm, self.T, self.D, self.L, self.M, self.F = (
            n,
            nm,
            tokens,
            width,
            local,
            feats,
            hidden,
        )
        self.H = local // HD
        self.HM = self.H * feats
        self.Tm = tokens // nm
        self.big = n > 8
        self.G8 = n * PAD
        used = hidden + hidden + local
        self.used = used
        self.rp = round_up((used + n - 1) // n, 16)
        self.rq = round_up((3 * width + n - 1) // n, 16)
        self.R = self.rp * n
        n2 = n // 2
        T, D, L, HM, Tm, R = self.T, self.D, self.L, self.HM, self.Tm, self.R
        vm = "vmem"
        states = (n, HM, SEG * HD)
        place = "hbm" if self.big else vm
        self.inputs = [
            ("tok", "hbm"),
            ("bkt", vm),
            ("cel", vm),
            ("feat", vm),
            ("wqkv", vm),
            ("g1", vm),
            ("b1", vm),
            ("ob", vm),
            ("g2", vm),
            ("b2", vm),
            ("db", vm),
            ("cot", "hbm"),
            ("ow", "hbm"),
            ("up", "hbm"),
            ("ub", "hbm"),
            ("dn", "hbm"),
        ]
        self.outputs = [
            ("out_o", "hbm", (T, D), BF),
            ("gtok_o", "hbm", (T, D), BF),
            ("ffg_o", "hbm", (n, self.rp, D), BF),
            ("qkvg_o", "hbm", (n, self.rq, L), BF),
            ("small_o", vm, (16, D), F32),
        ]
        big_states = [("sp", states), ("rb", states), ("sall", states), ("gall", states)]
        if self.big:
            self.outputs += [(name, "hbm", shape, BF) for name, shape in big_states]
        self.scratch = [
            ("wcat", (D, 4 * L), BF),
            ("f2", (L, HM), BF),
            ("wb", (HM, 2 * L), BF),
            ("ccb", (T, LANES), BF),
            ("oh2", (T, 2 * self.G8), BF),
            ("nm", (T, D), BF),
            ("qk", (2, T, L), BF),
            ("vv", (2, T, L), BF),
            ("qf", (T, HM), BF),
            ("kf", (T, HM), BF),
            ("ft", (HM, T), BF),
            ("tp", (n, PAD, HM), F32),
            ("trb", (n, PAD, HM), F32),
            ("tall", (n, PAD, HM), F32),
            ("gtall", (n, PAD, HM), F32),
            ("tot2", (2 * self.G8, HM), BF),
            ("acc", (HM, SEG * HD), F32),
            ("attf", (T, L), F32),
            ("inv", (T, L), F32),
            ("attb", (T, L), BF),
            ("arow", (nm, Tm, L), BF),
            ("wq_g", (nm, 3, D, L), BF),
            ("ow_g", (nm, L, D), BF),
            ("up_g", (nm, D, hidden), BF),
            ("ub_g", (nm, 1, hidden), F32),
            ("dn_g", (nm, hidden, D), BF),
            ("cotv", (Tm, D), BF),
            ("tokv", (Tm, D), BF),
            ("mid", (Tm, D), F32),
            ("nm2", (Tm, D), BF),
            ("nm2t", (D, Tm), BF),
            ("act", (Tm, hidden), BF),
            ("gp", (Tm, hidden), BF),
            ("bo", (Tm, D), F32),
            ("gn2", (Tm, D), F32),
            ("gb", (Tm, D), BF),
            ("outv", (Tm, D), BF),
            ("small", (16, D), F32),
            ("small_m", (nm, 16, D), F32),
            ("small_d", (n, 16, D), F32),
            ("ffp", (nm, used, D), BF),
            ("ffc", (2, used, D), BF),
            ("ffy", (R, D), BF),
            ("ffx", (n2, self.rp, D), BF),
            ("ffz", (n2, self.rp, D), BF),
            ("gas", (nm, Tm, L), BF),
            ("gar", (nm, Tm, L), BF),
            ("gad", (2, T, L), BF),
            ("gg", (2, T, L), BF),
            ("gd", (T, L), F32),
            ("grads", (3, T, L), BF),
            ("garr", (nm, 3, Tm, L), BF),
            ("qkvp", (n, self.rq, L), BF),
            ("qkvx", (n2, self.rq, L), BF),
            ("qkvz", (n2, self.rq, L), BF),
            ("gtv", (Tm, D), BF),
        ]
        if self.big:
            self.scratch += [("stage_a", (2, HM, SEG * HD), BF), ("stage_b", (2, HM, SEG * HD), BF)]
        else:
            self.scratch += [(name, shape, BF) for name, shape in big_states]
        self.sems = {
            "rs": n,
            "rst": n,
            "ag": n,
            "agt": n,
            "rs2": n,
            "rst2": n,
            "ag2": n,
            "agt2": n,
            "a2a": nm,
            "gaa": nm,
            "grq": nm,
            "grk": nm,
            "wy": 5,
            "wc": 10,
            "ffc": 2,
            "ffy": 1,
            "ffx": 1,
            "ffz": n2,
            "ffgz": n2,
            "ffgx": 1,
            "qx": 1,
            "qz": n2,
            "qgz": n2,
            "qgx": 1,
            "oy": 1,
            "oc": 2,
            "ty": 1,
            "tc": 2,
            "sm": nm,
            "sd": n,
        }
        self.local_sems = 16

    def names(self):
        return (
            [x[0] for x in self.inputs]
            + [x[0] for x in self.outputs]
            + [x[0] for x in self.scratch]
            + [f"{k}_{end}" for k in self.sems for end in ("s", "r")]
            + ["lsem"]
        )


def layer_kernel(plan, *refs):
    r = SimpleNamespace(**dict(zip(plan.names(), refs, strict=True)))
    n, nm, T, D, L, M, HM, Tm, H = (
        plan.n,
        plan.nm,
        plan.T,
        plan.D,
        plan.L,
        plan.M,
        plan.HM,
        plan.Tm,
        plan.H,
    )
    hidden = plan.F
    n2 = n // 2
    tiles = T // TILE
    me, m = lax.axis_index("dp"), lax.axis_index("mp")
    sib = m + 1 - 2 * lax.rem(m, 2)
    far = lax.rem(m + nm // 2, nm)
    farsib = lax.rem(sib + nm // 2, nm)
    xpart = me + 1 - 2 * lax.rem(me, 2)
    xme, zme = lax.rem(me, 2), me // 2

    def sem(name, index):
        return getattr(r, f"{name}_s").at[index], getattr(r, f"{name}_r").at[index]

    def copy(src, dst, name, sent, dp=None, mp=None, got=None):
        send, _ = sem(name, sent)
        _, recv = sem(name, sent if got is None else got)
        return pltpu.make_async_remote_copy(
            src_ref=src,
            dst_ref=dst,
            send_sem=send,
            recv_sem=recv,
            device_id=(me if dp is None else dp, m if mp is None else mp),
            device_id_type=MESH,
        )

    def local(src, dst, index):
        return pltpu.make_async_copy(src, dst, r.lsem.at[index])

    low = lane((1, LANES)) < HD

    barrier = pltpu.get_barrier_semaphore()

    def greet(k):
        pl.semaphore_signal(
            barrier, inc=1, device_id=(lax.rem(me + 1 + k, n), m), device_id_type=MESH
        )

    loop(n - 1, greet)
    for k in range(1, nm):
        pl.semaphore_signal(
            barrier, inc=1, device_id=(me, lax.rem(m + k, nm)), device_id_type=MESH
        )

    mine = rows_of(m, Tm)
    tok_in = local(r.tok, r.nm, 10)
    own_in = [local(r.cot.at[mine], r.cotv, 0), local(r.tok.at[mine], r.tokv, 11)]
    for c in [tok_in, *own_in]:
        c.start()

    r.wcat[:, 0:L] = r.wqkv[0]
    r.wcat[:, L : 2 * L] = r.wqkv[1]
    wv = r.wqkv[2].astype(F32)
    wv_rolled = roll_half(wv)
    r.wcat[:, 2 * L : 3 * L] = jnp.where(low, wv, wv_rolled).astype(BF)
    r.wcat[:, 3 * L : 4 * L] = jnp.where(low, wv_rolled, wv).astype(BF)
    feature_rows = r.feat[STEP % FEATS]
    r.f2[...] = jnp.zeros((L, HM), BF)
    for h in range(H):
        r.f2[h * HD : (h + 1) * HD, h * M : (h + 1) * M] = feature_rows
    r.wb[:, 0:L] = r.f2[...].astype(F32).T.astype(BF)
    head_of_row = lax.broadcasted_iota(jnp.int32, (HM, L), 0) // M
    r.wb[:, L : 2 * L] = jnp.where(head_of_row == lane((HM, L)) // HD, 1.0, 0.0).astype(BF)

    def ids(i):
        rows = rows_of(i, LANES)
        b, c = r.bkt[pl.ds(i, 1), :].astype(F32), r.cel[pl.ds(i, 1), :].astype(F32)
        square = (LANES, LANES)
        cell = jnp.broadcast_to(SEG * b + c, square).T - jnp.where(low, 0.0, 1.0)
        r.ccb[rows, :] = cell.astype(BF)
        padded = PAD * b + c
        column = jnp.broadcast_to(padded, square).T
        for block in range(2 * plan.G8 // LANES):
            number = (lane(square) + block * LANES) % plan.G8
            r.oh2[rows, block * LANES : (block + 1) * LANES] = jnp.where(
                column == number.astype(F32), 1.0, 0.0
            ).astype(BF)

    loop(T // LANES, ids)
    tok_in.wait()

    def phi(u):
        wide = u.astype(F32)
        squares = wide * wide
        first = jnp.sum(jnp.where(low, squares, 0.0), -1, keepdims=True)
        second = jnp.sum(jnp.where(low, 0.0, squares), -1, keepdims=True)
        projected = dot(u, r.f2[...]) * SCALE
        shift = jnp.where(lane((1, HM)) < M, first, second) * HALF_SQUARE
        return jnp.exp(projected - shift)

    def project(i):
        rows = rows_of(i, TILE)
        hat, _ = normalised(r.nm[rows, :].astype(F32))
        normed = (hat * r.g1[...] + r.b1[...]).astype(BF)
        r.nm[rows, :] = normed
        u = dot(normed, r.wcat[...]).astype(BF)
        q, k = u[:, 0:L], u[:, L : 2 * L]
        r.qk[0, rows, :], r.qk[1, rows, :] = q, k
        r.vv[0, rows, :], r.vv[1, rows, :] = u[:, 2 * L : 3 * L], u[:, 3 * L : 4 * L]
        r.qf[rows, :] = phi(q).astype(BF)
        features = phi(k)
        r.kf[rows, :] = features.astype(BF)
        r.ft[:, rows] = features.T.astype(BF)

    loop(tiles, project)

    pl.semaphore_wait(barrier, n - 1 + nm - 1)

    shards = [
        (r.wqkv, r.wq_g),
        (r.ow, r.ow_g),
        (r.up, r.up_g),
        (r.ub, r.ub_g),
        (r.dn, r.dn_g),
    ]
    own_copies, y_copies, core_copies = [], [], []
    for i, (src, dst) in enumerate(shards):
        own_copies.append(local(src, dst.at[m], 1 + i))
        y_copies.append(copy(src, dst.at[m], "wy", i, mp=far))
        core_copies.append(copy(src, dst.at[m], "wc", 2 * i, mp=sib))
    for c in own_copies + y_copies + core_copies:
        c.start()

    def state_pair(ref, p, stage):
        if plan.big:
            pltpu.sync_copy(ref.at[pl.ds(2 * p, 2)], stage)
            return stage
        return ref.at[pl.ds(2 * p, 2)]

    def masked_pair(rows, dup, p):
        code = r.ccb[rows, :]
        first = jnp.full((1, LANES), 1.0, F32) * (4 * p)
        left = jnp.where(code == first.astype(BF), dup, jnp.zeros_like(dup))
        right = jnp.where(code == (first + 2.0).astype(BF), dup, jnp.zeros_like(dup))
        return jnp.concatenate([left, right], 1)

    everything = pl.ds(0, T)

    def scatter_states(dup, name, name_t):
        def pair(kk):
            p = lax.rem(zme + 1 + kk, n2)
            staged = r.stage_a if plan.big else r.sp.at[pl.ds(2 * p, 2)]
            for h in range(H):
                hs = slice(h * M, (h + 1) * M)
                block = dot(r.ft[hs, :], masked_pair(everything, dup[h], p))
                staged[0, hs, :] = block[:, :LANES].astype(BF)
                staged[1, hs, :] = block[:, LANES:].astype(BF)
            if plan.big:
                pltpu.sync_copy(r.stage_a, r.sp.at[pl.ds(2 * p, 2)])
            for side in range(2):
                j = 2 * p + side

                @pl.when(j != me)
                def _():
                    copy(r.sp.at[j], r.rb.at[me], name, j, dp=j, got=me).start()
                    copy(r.tp.at[j], r.trb.at[me], name_t, j, dp=j, got=me).start()

        loop(n2, pair, unroll=False)

    def reduce_states(name, name_t, all_s, all_t, ag, agt):
        if plan.big:
            pltpu.sync_copy(r.sp.at[pl.ds(me, 1)], r.stage_b.at[pl.ds(0, 1)])
            r.acc[...] = r.stage_b[0].astype(F32)
        else:
            r.acc[...] = r.sp[me].astype(F32)
        all_t[me] = r.tp[me]

        def add(k):
            j = lax.rem(me + 1 + k, n)
            copy(r.sp.at[j], r.rb.at[j], name, j, dp=j).wait_recv()
            copy(r.tp.at[j], r.trb.at[j], name_t, j, dp=j).wait_recv()
            if plan.big:
                pltpu.sync_copy(r.rb.at[pl.ds(j, 1)], r.stage_b.at[pl.ds(0, 1)])
                r.acc[...] += r.stage_b[0].astype(F32)
            else:
                r.acc[...] += r.rb[j].astype(F32)
            all_t[me] += r.trb[j]

        loop(n - 1, add)
        if plan.big:
            r.stage_b[0] = r.acc[...].astype(BF)
            pltpu.sync_copy(r.stage_b.at[pl.ds(0, 1)], all_s.at[pl.ds(me, 1)])
        else:
            all_s[me] = r.acc[...].astype(BF)

        def send(k):
            j = lax.rem(me + 1 + k, n)
            copy(all_s.at[me], all_s.at[me], ag, j, dp=j, got=me).start()
            copy(all_t.at[me], all_t.at[me], agt, j, dp=j, got=me).start()

        loop(n - 1, send)

    def gathered_states(name, name_t, all_s, all_t, ag, agt):
        def wait(k):
            j = lax.rem(me + 1 + k, n)
            copy(all_s.at[j], all_s.at[j], ag, j, dp=j).wait_recv()
            copy(all_t.at[j], all_t.at[j], agt, j, dp=j).wait_recv()

        loop(n - 1, wait)

        def sent(k):
            j = lax.rem(me + 1 + k, n)
            copy(r.sp.at[j], r.rb.at[me], name, j, dp=j, got=me).wait_send()
            copy(r.tp.at[j], r.trb.at[me], name_t, j, dp=j, got=me).wait_send()
            copy(all_s.at[me], all_s.at[me], ag, j, dp=j, got=me).wait_send()
            copy(all_t.at[me], all_t.at[me], agt, j, dp=j, got=me).wait_send()

        loop(n - 1, sent)
        total = all_t[...].reshape(plan.G8, HM)
        top = total.astype(BF)
        r.tot2[0 : plan.G8, :] = top
        r.tot2[plan.G8 :, :] = (total - top.astype(F32)).astype(BF)

    r.tp[...] = dot_tn(r.oh2[:, : plan.G8], r.kf[...]).reshape(n, PAD, HM)
    scatter_states([r.vv[0], r.vv[1]], "rs", "rst")

    def turn(i):
        rows = rows_of(i, TILE)
        r.ft[:, rows] = r.qf[rows, :].astype(F32).T.astype(BF)

    loop(tiles, turn)
    onward = []
    for i, (_, dst) in enumerate(shards):
        copy(dst.at[far], dst.at[far], "wy", i, mp=far).wait_recv()
        c = copy(dst.at[far], dst.at[far], "wc", 2 * i + 1, mp=sib)
        c.start()
        onward.append(c)

    reduce_states("rs", "rst", r.sall, r.tall, "ag", "agt")
    gathered_states("rs", "rst", r.sall, r.tall, "ag", "agt")

    def select_heads(rows, left, all_s):
        code = r.ccb[rows, :].astype(F32)

        def pair(h, p, total):
            hs = slice(h * M, (h + 1) * M)
            blocks = state_pair(all_s, p, r.stage_a if plan.big else None)
            right = jnp.concatenate([blocks[0, hs, :], blocks[1, hs, :]], 1)
            product = dot(left[:, hs], right)
            first = jnp.full((1, LANES), 1.0, F32) * (4 * p)
            total = jnp.where(code == first, product[:, :LANES], total)
            return jnp.where(code == first + 2.0, product[:, LANES:], total)

        heads = []
        for h in range(H):
            total = jnp.zeros((left.shape[0], LANES), F32)
            if plan.big:
                total = lax.fori_loop(0, n2, functools.partial(pair, h), total)
            else:
                for p in range(n2):
                    total = pair(h, p, total)
            heads.append(total + roll_half(total))
        return jnp.where(low, heads[0], heads[1])

    def own_totals(rows):
        return dot(r.oh2[rows, :], r.tot2[...])

    def halves(first, second):
        return jnp.where(low, first, second)

    def attend(i):
        rows = rows_of(i, TILE)
        queries = r.qf[rows, :]
        numerator = select_heads(rows, queries, r.sall)
        product = queries.astype(F32) * own_totals(rows)
        denominator = halves(
            jnp.sum(product[:, :M], -1, keepdims=True),
            jnp.sum(product[:, M:], -1, keepdims=True),
        )
        attention = numerator / denominator
        r.attf[rows, :] = attention
        r.inv[rows, :] = 1.0 / denominator
        r.attb[rows, :] = attention.astype(BF)

    per_chunk = Tm // TILE
    chunk_order = [far, farsib, sib, m]

    def chunks(body, after):
        for k, target in enumerate(chunk_order):
            loop(per_chunk, lambda i, target=target: body(target * per_chunk + i))
            after(k, target)

    def send_attention(k, target):
        if k < nm - 1:
            copy(
                r.attb.at[rows_of(target, Tm)], r.arow.at[m], "a2a", target, mp=target, got=m
            ).start()
        else:
            r.arow[m] = r.attb[rows_of(m, Tm), :]

    chunks(attend, send_attention)

    for c in own_copies:
        c.wait()
    for i, (_, dst) in enumerate(shards):
        copy(dst.at[sib], dst.at[sib], "wc", 2 * i, mp=sib).wait_recv()
        copy(dst.at[farsib], dst.at[farsib], "wc", 2 * i + 1, mp=sib).wait_recv()
    for c in y_copies + core_copies + onward:
        c.wait_send()
    for c in own_in:
        c.wait()
    for target in chunk_order[: nm - 1]:
        copy(r.arow.at[target], r.arow.at[target], "a2a", target, mp=target).wait_recv()

    r.small[...] = jnp.zeros((16, D), F32)

    def project_out(i):
        rows = rows_of(i, TILE)
        columns = jnp.concatenate([r.arow[s, rows, :] for s in range(nm)], 1)
        branch = dot(columns, r.ow_g[...].reshape(D, D)).astype(BF).astype(F32)
        middle = r.tokv[rows, :].astype(F32) + branch + r.ob[...]
        r.mid[rows, :] = middle
        hat, _ = normalised(middle)
        normed = hat * r.g2[...] + r.b2[...]
        r.nm2[rows, :] = normed.astype(BF)
        r.nm2t[:, rows] = normed.T.astype(BF)
        r.small[0:1, :] += jnp.sum(r.cotv[rows, :].astype(F32), 0, keepdims=True)

    loop(Tm // TILE, project_out)

    def units(s):
        up, down = r.up_g[s], r.dn_g[s]

        def tile(i):
            rows = rows_of(i, TILE)
            preact = dot(r.nm2[rows, :], up) + r.ub_g[s]
            spread = 0.5 + 0.5 * lax.erf(preact * (0.5**0.5))
            active = (preact * spread).astype(BF)
            r.act[rows, :] = active
            slope = spread + preact * jnp.exp(preact * preact * -0.5) * 0.3989422804014327
            grad = (dot_nt(r.cotv[rows, :], down) * slope).astype(BF)
            r.gp[rows, :] = grad
            forward, backward = dot(active, down), dot_nt(grad, up)
            r.bo[rows, :] += forward
            r.gn2[rows, :] += backward
            r.small[pl.ds(8 + s, 1), :] += jnp.sum(grad.astype(F32), 0, keepdims=True)

        loop(Tm // TILE, tile)
        r.ffp[s, 0:hidden, :] = dot(r.nm2t[...], r.gp[...]).astype(BF)
        r.ffp[s, hidden : 2 * hidden, :] = dot_tn(r.act[...], r.cotv[...]).astype(BF)

    r.bo[...] = jnp.zeros((Tm, D), F32)
    r.gn2[...] = jnp.zeros((Tm, D), F32)
    lax.fori_loop(0, nm, lambda s, carry: (units(s), carry)[1], 0)

    def norm2_back(i):
        rows = rows_of(i, TILE)
        middle = r.mid[rows, :]
        r.outv[rows, :] = (middle + r.bo[rows, :] + r.db[...]).astype(BF)
        hat, scale = normalised(middle)
        upstream = r.gn2[rows, :]
        r.small[1:2, :] += jnp.sum(upstream * hat, 0, keepdims=True)
        r.small[2:3, :] += jnp.sum(upstream, 0, keepdims=True)
        grad = r.cotv[rows, :].astype(F32) + norm_back(upstream, hat, scale, r.g2[...])
        r.mid[rows, :] = grad
        r.small[3:4, :] += jnp.sum(grad, 0, keepdims=True)
        low_grad = grad.astype(BF)
        r.gb[rows, :] = low_grad
        back = dot_nt(low_grad, r.ow_g[...].reshape(D, D)).astype(BF)
        for s in range(nm):
            r.gas[s, rows, :] = back[:, s * L : (s + 1) * L]

    loop(Tm // TILE, norm2_back)
    for target in chunk_order[: nm - 1]:
        copy(r.gas.at[target], r.gar.at[m], "gaa", target, mp=target, got=m).start()
    r.gar[m] = r.gas[m]
    for s in range(nm):
        r.ffp[s, 2 * hidden : 2 * hidden + L, :] = dot_tn(r.arow[s], r.gb[...]).astype(BF)

    ff_core = [
        copy(r.ffp.at[sib], r.ffc.at[0], "ffc", 0, mp=sib),
        copy(r.ffp.at[farsib], r.ffc.at[1], "ffc", 1, mp=sib),
    ]
    out_mine = local(r.outv, r.out_o.at[mine], 6)
    out_y = copy(r.outv, r.out_o.at[mine], "oy", 0, mp=far)
    out_core = copy(r.outv, r.out_o.at[mine], "oc", 0, mp=sib)
    for c in [*ff_core, out_mine, out_core]:
        c.start()

    for target in chunk_order[: nm - 1]:
        copy(r.gar.at[target], r.gar.at[target], "gaa", target, mp=target).wait_recv()
    out_y.start()

    def grad_rows(i):
        rows = rows_of(i, TILE)
        s = i // per_chunk
        inner = rows_of(i - s * per_chunk, TILE)
        grad = r.gar[s, inner, :].astype(F32)
        inv = r.inv[rows, :]
        scaled = grad * inv
        g_roll, s_roll = roll_half(grad), roll_half(scaled)
        r.gad[0, rows, :] = halves(grad, g_roll).astype(BF)
        r.gad[1, rows, :] = halves(g_roll, grad).astype(BF)
        r.gg[0, rows, :] = halves(scaled, s_roll).astype(BF)
        r.gg[1, rows, :] = halves(s_roll, scaled).astype(BF)
        product = scaled * r.attf[rows, :]
        r.gd[rows, :] = -halves(
            jnp.sum(jnp.where(low, product, 0.0), -1, keepdims=True),
            jnp.sum(jnp.where(low, 0.0, product), -1, keepdims=True),
        )

    loop(tiles, grad_rows)

    def head_column(values, h):
        return values[:, h * HD : h * HD + 1]

    for h in range(H):
        column = r.gd[:, h * HD : h * HD + 1]
        top = column.astype(BF).astype(F32)
        upper = lane((1, 2 * plan.G8)) < plan.G8
        weights = r.oh2[...] * jnp.where(upper, top, column - top).astype(BF)
        summed = dot_tn(weights, r.qf[:, h * M : (h + 1) * M])
        summed = summed[: plan.G8] + summed[plan.G8 :]
        r.tp[:, :, h * M : (h + 1) * M] = summed.reshape(n, PAD, M)
    scatter_states([r.gg[0], r.gg[1]], "rs2", "rst2")

    def contract(rows, dup, all_s, h):
        hs = slice(h * M, (h + 1) * M)

        def pair(p, total):
            blocks = state_pair(all_s, p, r.stage_a if plan.big else None)
            right = jnp.concatenate([blocks[0, hs, :], blocks[1, hs, :]], 1)
            return total + dot_nt(masked_pair(rows, dup[h, rows, :], p), right)

        total = jnp.zeros((TILE, M), F32)
        if plan.big:
            return lax.fori_loop(0, n2, pair, total)
        for p in range(n2):
            total = pair(p, total)
        return total

    def feature_back(rows, which, grad_features):
        u = r.qk[which, rows, :]
        weighted = (grad_features * phi(u)).astype(BF)
        both = dot(weighted, r.wb[...])
        return (
            both[:, :L] * SCALE - both[:, L:] * u.astype(F32) * (SCALE * SCALE)
        ).astype(BF)

    def query_back(i):
        rows = rows_of(i, TILE)
        totals = own_totals(rows)
        inv, gd = r.inv[rows, :], r.gd[rows, :]
        parts = [
            contract(rows, r.gad, r.sall, h) * head_column(inv, h)
            + totals[:, h * M : (h + 1) * M] * head_column(gd, h)
            for h in range(H)
        ]
        r.grads[0, rows, :] = feature_back(rows, 0, jnp.concatenate(parts, 1))

    loop(tiles, query_back)
    for target in chunk_order[: nm - 1]:
        copy(
            r.grads.at[0, rows_of(target, Tm)], r.garr.at[m, 0], "grq", target, mp=target, got=m
        ).start()

    copy(r.ffp.at[m], r.ffc.at[0], "ffc", 0, mp=sib).wait_recv()
    copy(r.ffp.at[far], r.ffc.at[1], "ffc", 1, mp=sib).wait_recv()
    for c in ff_core:
        c.wait_send()
    step = 128

    def core_sum(i):
        rows = rows_of(i, step)
        r.ffp[far, rows, :] = (
            r.ffp[far, rows, :].astype(F32) + r.ffc[1, rows, :].astype(F32)
        ).astype(BF)

    loop(plan.used // step, core_sum)
    used = pl.ds(0, plan.used)
    ff_y = copy(r.ffp.at[far], r.ffy.at[used], "ffy", 0, mp=far)
    ff_y.start()

    reduce_states("rs2", "rst2", r.gall, r.gtall, "ag2", "agt2")

    ff_y.wait_recv()
    ff_y.wait_send()

    def y_sum(i):
        rows = rows_of(i, step)
        r.ffy[rows, :] = (
            r.ffp[m, rows, :].astype(F32)
            + r.ffc[0, rows, :].astype(F32)
            + r.ffy[rows, :].astype(F32)
        ).astype(BF)

    loop(plan.used // step, y_sum)

    class Reduction:
        def __init__(self, source, rx, rz, out, names, rows, lsem):
            self.source, self.rx, self.rz, self.out = source, rx, rz, out
            self.x, self.z, self.gz, self.gx = names
            self.rows, self.lsem = rows, lsem

        def block(self, k):
            return self.source(xme * n2 + k)

        def start(self):
            first = self.source(pl.ds((1 - xme) * n2, n2))
            self.sent = copy(first, self.rx, self.x, 0, dp=xpart)
            self.sent.start()

        def scatter(self):
            self.sent.wait()

            def add(k):
                ref = self.block(k)
                ref[...] = (ref[...].astype(F32) + self.rx[k].astype(F32)).astype(BF)

            loop(n2, add)

            def send(k):
                z = lax.rem(zme + 1 + k, n2)
                copy(self.block(z), self.rz.at[zme], self.z, z, dp=2 * z + xme, got=zme).start()

            loop(n2 - 1, send)

        def gather(self):
            own = self.block(zme)

            total = own[...].astype(F32)

            def take(k, total):
                z = lax.rem(zme + 1 + k, n2)
                copy(self.block(z), self.rz.at[z], self.z, z, dp=2 * z + xme).wait()
                return total + self.rz[z].astype(F32)

            if n2 <= 4:
                for k in range(n2 - 1):
                    total = take(k, total)
            else:
                total = lax.fori_loop(0, n2 - 1, take, total)
            own[...] = total.astype(BF)
            spot = self.out.at[xme * n2 + zme]
            self.kept = local(own, spot, self.lsem)
            self.kept.start()

            def send(k):
                z = lax.rem(zme + 1 + k, n2)
                copy(own, spot, self.gz, z, dp=2 * z + xme, got=zme).start()

            loop(n2 - 1, send)

        def spread(self):
            own = self.block(zme)
            self.kept.wait()

            def wait(k):
                z = lax.rem(zme + 1 + k, n2)
                copy(own, self.out.at[xme * n2 + z], self.gz, z, dp=2 * z + xme).wait()

            loop(n2 - 1, wait)
            half = self.out.at[pl.ds(xme * n2, n2)]
            self.last = copy(half, half, self.gx, 0, dp=xpart)
            self.last.start()

        def finish(self):
            half = self.out.at[pl.ds((1 - xme) * n2, n2)]
            copy(half, half, self.gx, 0, dp=xpart).wait_recv()
            self.last.wait_send()

    rp, rq = plan.rp, plan.rq

    def ff_block(index):
        return r.ffy.reshape(n, rp, D).at[index]

    ff = Reduction(ff_block, r.ffx, r.ffz, r.ffg_o, ("ffx", "ffz", "ffgz", "ffgx"), rp, 7)
    ff.start()

    out_far = rows_of(far, Tm)
    copy(r.outv, r.out_o.at[out_far], "oy", 0, mp=far).wait_recv()
    out_on = copy(r.out_o.at[out_far], r.out_o.at[out_far], "oc", 1, mp=sib)
    out_on.start()

    gathered_states("rs2", "rst2", r.gall, r.gtall, "ag2", "agt2")

    def key_back(i):
        rows = rows_of(i, TILE)
        totals = own_totals(rows)
        parts = [
            contract(rows, r.vv, r.gall, h) + totals[:, h * M : (h + 1) * M] for h in range(H)
        ]
        r.grads[1, rows, :] = feature_back(rows, 1, jnp.concatenate(parts, 1))
        r.grads[2, rows, :] = select_heads(rows, r.kf[rows, :], r.gall).astype(BF)

    def send_grads(k, target):
        if k < nm - 1:
            spot = rows_of(target, Tm)
            copy(
                r.grads.at[pl.ds(1, 2), spot], r.garr.at[m, pl.ds(1, 2)], "grk", target, mp=target, got=m
            ).start()
        else:
            for a in range(3):
                r.garr[m, a] = r.grads[a, rows_of(m, Tm), :]

    chunks(key_back, send_grads)
    ff.scatter()

    for a in range(3):
        part = dot_tn(r.nm[...], r.grads[a]).astype(BF)
        r.qkvp.reshape(n * rq, L)[a * D : (a + 1) * D, :] = part
    qkv = Reduction(
        lambda index: r.qkvp.at[index], r.qkvx, r.qkvz, r.qkvg_o, ("qx", "qz", "qgz", "qgx"), rq, 8
    )
    qkv.start()

    for target in chunk_order[: nm - 1]:
        copy(r.garr.at[target, 0], r.garr.at[target, 0], "grq", target, mp=target).wait_recv()
        pair = r.garr.at[target, pl.ds(1, 2)]
        copy(pair, pair, "grk", target, mp=target).wait_recv()

    def norm1_back(i):
        rows = rows_of(i, TILE)
        upstream = jnp.zeros((TILE, D), F32)
        for s in range(nm):
            left = jnp.concatenate([r.garr[s, a, rows, :] for a in range(3)], 1)
            right = jnp.concatenate([r.wq_g[s, a] for a in range(3)], 1)
            upstream += dot_nt(left, right)
        upstream = upstream.astype(BF).astype(F32)
        hat, scale = normalised(r.tokv[rows, :].astype(F32))
        r.small[4:5, :] += jnp.sum(upstream * hat, 0, keepdims=True)
        r.small[5:6, :] += jnp.sum(upstream, 0, keepdims=True)
        r.gtv[rows, :] = (r.mid[rows, :] + norm_back(upstream, hat, scale, r.g1[...])).astype(BF)

    loop(Tm // TILE, norm1_back)
    tok_mine = local(r.gtv, r.gtok_o.at[mine], 9)
    tok_y = copy(r.gtv, r.gtok_o.at[mine], "ty", 0, mp=far)
    tok_core = copy(r.gtv, r.gtok_o.at[mine], "tc", 0, mp=sib)
    for c in (tok_y, tok_core, tok_mine):
        c.start()

    small_m = []
    for k, target in enumerate(chunk_order[: nm - 1]):
        c = copy(r.small, r.small_m.at[m], "sm", target, mp=target, got=m)
        c.start()
        small_m.append(c)
    ff.gather()
    qkv.scatter()
    total = r.small[...]
    for target in chunk_order[: nm - 1]:
        copy(r.small, r.small_m.at[target], "sm", target, mp=target).wait_recv()
        total += r.small_m[target]
    for c in small_m:
        c.wait_send()
    r.small_m[m] = total

    def small_send(k):
        j = lax.rem(me + 1 + k, n)
        copy(r.small_m.at[m], r.small_d.at[me], "sd", j, dp=j, got=me).start()

    loop(n - 1, small_send)
    qkv.gather()
    ff.spread()
    qkv.spread()
    r.small_o[...] = r.small_m[m]

    def small_take(k):
        j = lax.rem(me + 1 + k, n)
        copy(r.small_m.at[m], r.small_d.at[j], "sd", j, dp=j).wait()
        r.small_o[...] += r.small_d[j]

    loop(n - 1, small_take)
    r.small_o[6:7, :] = r.small_o[pl.ds(8 + m, 1), :]

    tok_far = rows_of(far, Tm)
    copy(r.gtv, r.gtok_o.at[tok_far], "ty", 0, mp=far).wait_recv()
    tok_on = copy(r.gtok_o.at[tok_far], r.gtok_o.at[tok_far], "tc", 1, mp=sib)
    tok_on.start()
    ff.finish()
    qkv.finish()
    for name, here in (("oc", r.out_o), ("tc", r.gtok_o)):
        for index, owner in enumerate((sib, farsib)):
            spot = here.at[rows_of(owner, Tm)]
            copy(spot, spot, name, index, mp=sib).wait_recv()
    for c in (out_y, out_core, out_on, tok_y, tok_core, tok_on):
        c.wait_send()
    for c in (out_mine, tok_mine):
        c.wait()
    for target in chunk_order[: nm - 1]:
        copy(
            r.attb.at[rows_of(target, Tm)], r.arow.at[m], "a2a", target, mp=target
        ).wait_send()
        copy(r.gas.at[target], r.gar.at[m], "gaa", target, mp=target).wait_send()
        spot = rows_of(target, Tm)
        copy(r.grads.at[0, spot], r.garr.at[m, 0], "grq", target, mp=target).wait_send()
        copy(
            r.grads.at[pl.ds(1, 2), spot], r.garr.at[m, pl.ds(1, 2)], "grk", target, mp=target
        ).wait_send()


def per_device(
    n,
    nm,
    tokens,
    cotangent,
    bucket,
    cell,
    features,
    qkv_weight,
    out_weight,
    out_bias,
    norm1_gain,
    norm1_bias,
    norm2_gain,
    norm2_bias,
    up_weight,
    up_bias,
    down_weight,
    down_bias,
):
    count, width = tokens.shape
    local, hidden = qkv_weight.shape[2], up_weight.shape[1]
    plan = Plan(n, nm, count, width, local, features.shape[2], hidden)
    spaces = {"vmem": pltpu.VMEM, "hbm": pl.ANY}
    line = lambda v: v.reshape(1, -1)
    grid_ids = (count // LANES, LANES)
    outs = pl.pallas_call(
        functools.partial(layer_kernel, plan),
        out_shape=[jax.ShapeDtypeStruct(s, d) for _, _, s, d in plan.outputs],
        in_specs=[pl.BlockSpec(memory_space=spaces[k]) for _, k in plan.inputs],
        out_specs=[pl.BlockSpec(memory_space=spaces[k]) for _, k, _, _ in plan.outputs],
        scratch_shapes=[pltpu.VMEM(s, d) for _, s, d in plan.scratch]
        + [pltpu.SemaphoreType.DMA((c,)) for c in plan.sems.values() for _ in range(2)]
        + [pltpu.SemaphoreType.DMA((plan.local_sems,))],
        compiler_params=pltpu.CompilerParams(
            collective_id=1, has_side_effects=True, vmem_limit_bytes=63 << 20
        ),
        name="performer_layer",
    )(
        tokens,
        bucket.reshape(grid_ids),
        cell.reshape(grid_ids),
        features,
        qkv_weight,
        line(norm1_gain),
        line(norm1_bias),
        line(out_bias),
        line(norm2_gain),
        line(norm2_bias),
        line(down_bias),
        cotangent,
        out_weight,
        up_weight,
        line(up_bias),
        down_weight,
    )
    output, grad_tokens, ff, qkv, small = outs[:5]
    ff = ff.reshape(-1, width).astype(F32)
    qkv = qkv.reshape(-1, local)[: 3 * width].astype(F32).reshape(3, width, local)
    return (
        output,
        grad_tokens.astype(F32),
        qkv,
        ff[2 * hidden : 2 * hidden + local],
        small[3],
        small[4],
        small[5],
        small[1],
        small[2],
        ff[:hidden],
        small[6],
        ff[hidden : 2 * hidden],
        small[0],
    )


def solution(mesh):
    return jax.shard_map(
        functools.partial(per_device, mesh.shape["dp"], mesh.shape["mp"]),
        mesh=mesh,
        in_specs=(
            P("dp", None),
            P("dp", None),
            P("dp", None),
            P("dp"),
            P(),
            P(None, None, "mp"),
            P("mp", None),
            P(),
            P(),
            P(),
            P(),
            P(),
            P(None, "mp"),
            P("mp"),
            P("mp", None),
            P(),
        ),
        out_specs=(
            P("dp", None),
            P("dp", None),
            P(None, None, "mp"),
            P("mp", None),
            P(),
            P(),
            P(),
            P(),
            P(),
            P(None, "mp"),
            P("mp"),
            P("mp", None),
            P(),
        ),
        check_vma=False,
    )
```

time: 1320 us -> 233 us (0.18); the launches traced: 1300 us -> 229 us
  waiting for transfers between devices: 698 us -> 0 us
  blocking collectives: 286 us -> 0 us
  Pallas kernels: 0 us -> 218 us
  matrix products: 143 us -> 0 us
  other arithmetic: 66.3 us -> 5.12 us
  local copies, waits for them, and re-layouts: 66.1 us -> 5.25 us
  starting transfers between devices: 25.8 us -> 0 us
  between operations: 15.4 us -> 0.68 us
    psum x2 -> x0, waiting for transfers between devices: 429 us -> none  [the longest x1 275 us: per_device(): lax.psum((grad_qkv_weight, grad_out_weight, grad_out_bias, grad_norm1_gai...]
    all_to_all x4 -> x0, waiting for transfers between devices: 269 us -> none  [the longest x2 180 us: home_rows(): lax.all_to_all(partial_rows, 'dp', split_axis=0, concat_axis=0, tiled=True)]
    pallas_call x0 -> x1, Pallas kernels: none -> 218 us  [per_device(): pl.pallas_call(functools.partial(layer_kernel, plan), out_shape=[jax.Shap...]
    psum x3 -> x0, blocking collectives: 187 us -> none  [the longest x2 153 us: home_rows(): return lax.psum(returned[slot_index], 'mp').astype(jnp.bfloat16)]
    dot_general x33 -> x0, matrix products: 139 us -> none  [the longest x2 16.4 us: per_device(): jnp.einsum('peo,exo->pex', numer_masked, cell_states[part_index], precisi...]
    all_to_all x1 -> x0, blocking collectives: 98.8 us -> none  [per_device(): lax.all_to_all(to_slots(grad_branch), 'dp', split_axis=0, concat_axis=0,...]
    reduce_sum x14 -> x0, other arithmetic: 31.9 us -> none  [the longest x3 11.6 us: layer_norm(): return centred * lax.rsqrt(spread + 1e-05) * norm_gain + norm_bias]
    scatter x2 -> x0, other arithmetic: 26.9 us -> none  [to_slots(): jnp.zeros((slots,) + rows.shape[1:], rows.dtype).at[slot_index].set(rows)]
  transfers between devices with their start and end apart: 6 -> 0, of which waited for: 4 -> 0; matrix products, arithmetic and copies ran while one was open for 2% -> 0% of each run, Pallas kernels for 0% -> 0%
where the time goes in v1:
time: 233 us; the launch traced here: 229 us
  Pallas kernels  218 us (94%)
  local copies, waits for them, and re-layouts  5.25 us (2%)
  other arithmetic  5.12 us (2%)
    pallas_call x1, Pallas kernels, per_device(): pl.pallas_call(functools.partial(layer_kernel, plan), out_shape=[jax.Shap...  218 us

profile of v1, /device:TPU:12, one launch (start us, length us, event | category | flops | bytes accessed | tf_op | source)
XLA Modules:
  0.0 229.2 jit_solution(16568128770597146661)
XLA Ops:
  0.7 218.1 %performer_layer.1 = (bf16[2048,512]{1,0:T(8,128)(2,1)}, bf16[2048,512]{1,0:T(8,128)(2,1)}, bf16[8,144,512]{2,1,0:T(8,128)(2,1)}, bf16[8,192,128]{2,1,0:T(8,128)(2,1)}, f32[16,512]{1,0:T(8,128)}) custom-call(bf16[2048,512]{1,0:T(8,128)(2,1)} %refs_0_.1, s32[16,128]{1,0:T(8,128)} %bitcast.22, s32[16,128]{1,0:T(8,128)} %bitcast.23, ...), custom_call_target="tpu_custom_call" | custom-call | tf_op jit(solution)/shard_map/performer_layer/pallas_call | solution.py:975
  218.8 1.6 fusion.1
  220.3 1.6 bitcast_convert_fusion
  221.9 0.0 copy-start
  221.9 1.5 fusion
  223.4 0.7 slice.40
  224.2 0.1 copy-done
  224.3 0.0 copy-start.2
  224.3 0.0 copy-start.1
  224.3 2.6 %convert_element_type.16 = f32[2048,512]{1,0:T(8,128)} convert(bf16[2048,512]{1,0:T(8,128)(2,1)S(1)} %copy-done) | non-fusion elementwise | flops 1048576 | bytes 6291456 | tf_op jit(solution)/shard_map/convert_element_type | solution.py:1010
  226.9 0.0 copy-done.2
  226.9 0.9 convert.3
  227.8 0.0 copy-done.1
  227.8 1.3 copy.30
Async XLA Ops:
  221.9 2.4 %copy-start = (bf16[2048,512]{1,0:T(8,128)(2,1)S(1)}, bf16[2048,512]{1,0:T(8,128)(2,1)}, u32[]{:S(2)}) copy-start(bf16[2048,512]{1,0:T(8,128)(2,1)} %get-tuple-element.19) | copy-start | bytes 6291460
  224.3 2.6 %copy-start.2 = (bf16[8,192,128]{2,1,0:T(8,128)(2,1)S(1)}, bf16[8,192,128]{2,1,0:T(8,128)(2,1)}, u32[]{:S(2)}) copy-start(bf16[8,192,128]{2,1,0:T(8,128)(2,1)} %get-tuple-element.20) | copy-start | bytes 1179652
  224.3 3.5 %copy-start.1 = (bf16[2048,512]{1,0:T(8,128)(2,1)S(1)}, bf16[2048,512]{1,0:T(8,128)(2,1)}, u32[]{:S(2)}) copy-start(bf16[2048,512]{1,0:T(8,128)(2,1)} %get-tuple-element.45) | copy-start | bytes 6291460
